TPU v7x, 256 devices: a whole 4x4x8 slice. The times are simulated.
256 devices in a mesh: row: 8 (over z), col: 32 (over x, y, core).
Axes of the slice: x: 4, y: 4, z: 8, core: 2. Of those that a mesh axis runs over, the one named last changes fastest.
Arguments:
- a_trail: float32 [16384, 16384], P('row', 'col'), may hold values from -60 to 60, as said below
- a_panel: float32 [16384, 256], P(('row', 'col')), may hold values from -6 to 6
- l_panel: float32 [16384, 256], P(('row', 'col')), may hold values from -0.5 to 0.5
- a_diag: float32 [256, 256], replicated, may hold values from -60 to 60, as said below
- l_inverse: float32 [256, 256], replicated, may hold values from -4 to 4, as said below
Outputs:
- trail_out: float32 [16384, 16384], P('row', 'col')
- panel_out: float32 [16384, 256], P(('row', 'col'))
Inputs may be any that keep to these rules, and one draw needn't show every extreme that they name: `a_trail`: symmetric. `a_diag`: symmetric. `l_inverse`: lower triangular with a positive diagonal.
All inputs are finite; a program needn't handle non-finite values.
Results may differ from a plain program's by a relative error of at most 0.0003.
Values sent between devices are 32-bit elements; how exact they have to be, the bound alone decides.
No kernel may reach another device: no remote copies, remote signals or barrier semaphores. Data moves between devices by JAX's collectives and lax.ppermute only.
A program may use at most 64 MiB of HBM per device.

v0:
```python
import jax
import jax.numpy as jnp
from jax import lax
from jax.sharding import PartitionSpec as P

NS_STEPS = 8


def from_root(block, axis, owner):
    block = jnp.where(lax.axis_index(axis) == owner, block, jnp.zeros_like(block))
    return lax.psum(block, axis)


def product(left, right):
    return jnp.dot(left, right, precision=lax.Precision.HIGHEST, preferred_element_type=jnp.float32)


def newton_inverse(matrix):
    identity = jnp.eye(matrix.shape[0], dtype=jnp.float32)
    approx = identity
    for repeat in range(NS_STEPS):
        approx = product(approx, 2.0 * identity - product(matrix, approx))
    return approx


def right_solve(factor, values):
    return lax.linalg.triangular_solve(
        factor, values, left_side=False, lower=True, transpose_a=True
    )


def shards(a_trail, a_panel, l_panel, a_diag, l_inverse):
    row_dev, col_dev = a_trail.shape
    block_width = a_diag.shape[0]
    row_index = lax.axis_index("row")
    col_index = lax.axis_index("col")
    owner_row = col_index * col_dev // row_dev
    offset = col_index * col_dev - owner_row * row_dev
    a11_new = product(product(l_inverse, a_diag), l_inverse.T)
    solved = product(a_panel, l_inverse.T)
    half_term = 0.5 * product(l_panel, a11_new)
    first_y = solved - half_term
    panel_out = first_y - half_term
    y_rows, l_rows = (
        lax.all_gather(first_y, "col", axis=0, tiled=True),
        lax.all_gather(l_panel, "col", axis=0, tiled=True),
    )
    stacked = jnp.stack(
        (
            lax.dynamic_slice_in_dim(y_rows, offset, col_dev, 0),
            lax.dynamic_slice_in_dim(l_rows, offset, col_dev, 0),
        )
    )
    received = from_root(stacked, "row", owner_row)
    y_cols = received[0]
    l_cols = received[1]
    updated = a_trail - (product(y_rows, l_cols.T) + product(l_rows, y_cols.T))
    got_panel = from_root(updated[:, :block_width], "col", 0)
    global_rows = row_index * row_dev + lax.iota(jnp.int32, row_dev)
    keep_mask = (global_rows >= block_width)[:, None]
    next_panel = jnp.where(keep_mask, got_panel, 0.0)
    picker = (
        global_rows[:, None] - block_width == lax.iota(jnp.int32, block_width)[None, :]
    ).astype(jnp.float32)
    gram, top_block = lax.psum(
        (product(next_panel.T, next_panel), product(picker.T, next_panel)), "row"
    )
    factor = jnp.linalg.cholesky(gram)
    q_rows = right_solve(factor, next_panel)
    q_top = right_solve(factor, top_block)
    identity = jnp.eye(block_width, dtype=jnp.float32)
    g_inverse = newton_inverse(identity + q_top).T
    refl_rows = q_rows + picker
    refl_cols = from_root(lax.dynamic_slice_in_dim(refl_rows, offset, col_dev, 0), "row", owner_row)
    x_rows = product(lax.psum(product(updated, refl_cols), "col"), g_inverse)
    m_core = product(g_inverse.T, lax.psum(product(refl_rows.T, x_rows), "row"))
    z_rows = x_rows - 0.5 * product(refl_rows, m_core)
    z_cols = from_root(lax.dynamic_slice_in_dim(z_rows, offset, col_dev, 0), "row", owner_row)
    trail_out = updated - (product(z_rows, refl_cols.T) + product(refl_rows, z_cols.T))
    return (trail_out, panel_out)


def solution(mesh):
    return jax.shard_map(
        shards,
        mesh=mesh,
        in_specs=(P("row", "col"), P(("row", "col"), None), P(("row", "col"), None), P(), P()),
        out_specs=(P("row", "col"), P(("row", "col"), None)),
        check_vma=False,
    )
```

profile of v0, /device:TPU:2, one launch (start us, length us, event | category | flops | bytes accessed | tf_op | source)
XLA Modules:
  0.0 843.6 jit_solution(7050816020331745766)
XLA Ops:
  7.2 0.9 copy-done
  8.1 1.3 fusion.23
  9.5 0.4 fusion.24
  9.9 1.1 fusion.3
  11.0 1.9 fusion.22
  12.9 0.7 all-gather.5.cloned.1.call-update
  13.7 50.7 %all-gather.3.cloned.1.call-done = f32[2048,256]{1,0:T(8,128)} async-done(((f32[64,256]{1,0:T(8,128)}), f32[2048,256]{1,0:T(8,128)}) %all-gather.3.cloned.1.call-update) | async-done | bytes 2097168 | tf_op jit(solution)/shard_map/all_gather | solution.py:45
  64.4 1.1 dynamic-slice_bitcast_fusion.1
  65.5 49.6 %all-gather.5.cloned.1.call-done = f32[2048,256]{1,0:T(8,128)} async-done(((f32[64,256]{1,0:T(8,128)}), f32[2048,256]{1,0:T(8,128)}) %all-gather.5.cloned.1.call-update) | async-done | bytes 2097168 | tf_op jit(solution)/shard_map/all_gather | solution.py:46
  115.1 1.1 dynamic-slice_bitcast_fusion
  116.2 1.0 maximum_select_fusion
  117.3 76.4 %all-reduce.10.cloned.1.call-done = f32[2,512,256]{2,1,0:T(8,128)} async-done(((f32[2,512,256]{2,1,0:T(8,128)}), f32[2,512,256]{2,1,0:T(8,128)}) %all-reduce.10.cloned.1.call-update) | async-done | bytes 1048592 | tf_op jit(solution)/shard_map/psum | solution.py:11
  193.7 4.7 fusion.7
  198.4 4.8 fusion
  203.2 2.0 copy-done.1
  205.2 1.6 slice_select_fusion
  207.1 115.2 %all-reduce.12.cloned.1.call-done = f32[2048,256]{1,0:T(8,128)} async-done(((f32[2048,256]{1,0:T(8,128)}), f32[2048,256]{1,0:T(8,128)}) %all-reduce.12.cloned.1.call-update) | async-done | bytes 2097168 | tf_op jit(solution)/shard_map/psum | solution.py:11
  322.3 1.9 broadcast_select_fusion
  324.2 4.2 fusion.25
  328.5 2.1 fusion.2
  330.6 70.8 %all-reduce.14.cloned.1.call-done = f32[256,256]{0,1:T(8,128)} async-done(((f32[256,256]{0,1:T(8,128)}), f32[256,256]{0,1:T(8,128)}) %all-reduce.14.cloned.1.call-update) | async-done | bytes 262160 | tf_op jit(solution)/shard_map/psum | solution.py:65
  401.4 1.1 copy.9
  402.5 1.0 fusion.8
  403.5 11.7 %cholesky.50 = f32[128,128]{1,0:T(8,128)S(1)} custom-call(f32[128,128]{1,0:T(8,128)S(1)} %cholesky.118), custom_call_target="Cholesky" | custom-call | tf_op jit(solution)/shard_map/jit(cholesky)/cholesky | solution.py:68
  415.3 9.8 %custom-call.16 = f32[1,128,128]{1,2,0:T(8,128)S(1)} custom-call(f32[1,128,128]{2,1,0:T(8,128)S(1)} %get-tuple-element.25), custom_call_target="InvertDiagBlocksLowerTriangular" | custom-call | tf_op jit(solution)/shard_map/jit(cholesky)/cholesky | solution.py:68
  425.6 11.7 %cholesky.105 = f32[128,128]{1,0:T(8,128)S(1)} custom-call(f32[128,128]{1,0:T(8,128)S(1)} %convolution_subtract_fusion.10), custom_call_target="Cholesky" | custom-call | tf_op jit(solution)/shard_map/jit(cholesky)/cholesky | solution.py:68
  437.3 0.7 compare_reduce_fusion
  439.3 4.0 while.1
  439.5 0.6 fusion.94
  440.1 1.3 bitcast_dynamic-update-slice_fusion.2
  441.4 0.6 fusion.94
  442.0 1.3 bitcast_dynamic-update-slice_fusion.2
  443.3 19.7 %custom-call.17 = f32[2,128,128]{1,2,0:T(8,128)S(1)} custom-call(f32[2,128,128]{2,1,0:T(8,128)S(1)} %get-tuple-element.9), custom_call_target="InvertDiagBlocksLowerTriangular" | custom-call | tf_op jit(solution)/shard_map/triangular_solve | solution.py:27
  463.0 1.1 fusion.4
  464.1 1.8 convolution_subtract_fusion
  465.9 1.1 fusion.16
  467.3 0.9 dynamic-slice_select_fusion.1
  468.5 73.0 %all-reduce.22.cloned.1.call-done = (f32[512,256]{0,1:T(8,128)}, f32[256,256]{1,0:T(8,128)}) async-done(((f32[512,256]{0,1:T(8,128)}, f32[256,256]{1,0:T(8,128)}), (f32[512,256]{0,1:T(8,128)}, f32[256,256]{1,0:T(8,128)})) %all-reduce.22.cloned.1.call-update) | async-done | bytes 786448 | tf_op jit(solution)/shard_map/psum | solution.py:11
  541.5 1.2 fusion.10
  542.7 1.3 convolution_subtract_fusion.9
  545.0 0.4 convolution_subtract_fusion.7
  545.8 0.4 convolution_subtract_fusion.6
  546.2 0.4 fusion.28
  546.6 0.4 convolution_subtract_fusion.5
  547.4 0.4 convolution_subtract_fusion.4
  548.2 1.1 convolution_subtract_fusion.3
  549.3 4.9 fusion.26
  554.2 0.5 all-reduce.18.cloned.1.call-start
  554.7 1.3 fusion.31
  556.0 0.4 convolution_subtract_fusion.2
  556.8 0.4 convolution_subtract_fusion.1
  557.6 112.1 %all-reduce.16.cloned.1.call-done = f32[2048,256]{1,0:T(8,128)} async-done(((f32[2048,256]{1,0:T(8,128)}), f32[2048,256]{1,0:T(8,128)}) %all-reduce.16.cloned.1.call-update) | async-done | bytes 2097168 | tf_op jit(solution)/shard_map/psum | solution.py:75
  669.7 3.5 fusion.34
  673.2 1.3 copy-done.3
  674.6 2.6 fusion.35
  677.4 2.9 copy.13
  680.3 69.8 %all-reduce.18.cloned.1.call-done = f32[256,256]{1,0:T(8,128)} async-done(((f32[256,256]{1,0:T(8,128)}), f32[256,256]{1,0:T(8,128)}) %all-reduce.18.cloned.1.call-update) | async-done | bytes 262160 | tf_op jit(solution)/shard_map/psum | solution.py:76
  750.1 1.3 fusion.36
  751.5 3.8 fusion.1
  755.3 1.3 copy-done.4
  756.6 0.8 dynamic-slice_select_fusion
  757.4 9.9 %fusion.37 = f32[2048,512]{1,0:T(8,128)} fusion(f32[2048,256]{0,1:T(8,128)} %copy-done.4, f32[512,256]{0,1:T(8,128)S(1)} %copy-done.8), kind=kOutput, calls=%fused_computation.84 | convolution fusion | flops 3221225472 | bytes 6815744 | tf_op jit(solution)/shard_map/dot_general | solution.py:15
  767.4 62.0 %all-reduce.20.cloned.1.call-done = f32[512,256]{0,1:T(8,128)} async-done(((f32[512,256]{0,1:T(8,128)}), f32[512,256]{0,1:T(8,128)}) %all-reduce.20.cloned.1.call-update) | async-done | bytes 524304 | tf_op jit(solution)/shard_map/psum | solution.py:11
  829.4 7.5 add_subtract_fusion
  (54 shorter events, 4.9 us)
Async XLA Ops:
  7.2 1.0 copy-start
  7.2 57.2 %all-gather.3.cloned.1.call-start = ((), (), s32[]{:S(2)}) async-start(), calls=%async_computation | async-start | bytes 2162688 | tf_op jit(solution)/shard_map/all_gather | solution.py:45
  12.9 102.2 %all-gather.5.cloned.1.call-start = ((), (), s32[]{:S(2)}) async-start(), calls=%async_computation.1 | async-start | bytes 2162688 | tf_op jit(solution)/shard_map/all_gather | solution.py:46
  13.6 180.0 %all-reduce.10.cloned.1.call-start = ((), (), s32[]{:S(2)}) async-start(), calls=%async_computation.2 | async-start | bytes 2097152 | tf_op jit(solution)/shard_map/psum | solution.py:11
  65.5 128.2 %copy-start.6 = (f32[2048,256]{1,0:T(8,128)S(1)}, f32[2048,256]{1,0:T(8,128)}, u32[]{:S(2)}) copy-start(f32[2048,256]{1,0:T(8,128)} %all-gather.3.cloned.1.call-done) | copy-start | bytes 6291460
  117.3 205.0 %all-reduce.12.cloned.1.call-start = ((), (), s32[]{:S(2)}) async-start(), calls=%async_computation.3 | async-start | bytes 4194304 | tf_op jit(solution)/shard_map/psum | solution.py:11
  193.7 4.7 copy-start.5
  193.7 4.7 copy-start.7
  203.2 2.0 copy-start.1
  206.8 194.6 %all-reduce.14.cloned.1.call-start = ((), (), s32[]{:S(2)}) async-start(), calls=%async_computation.4 | async-start | bytes 524288 | tf_op jit(solution)/shard_map/psum | solution.py:65
  328.4 213.1 %all-reduce.22.cloned.1.call-start = ((), (), s32[]{:S(2)}) async-start(), calls=%async_computation.8 | async-start | bytes 1572864 | tf_op jit(solution)/shard_map/psum | solution.py:11
  468.2 201.5 %all-reduce.16.cloned.1.call-start = ((), (), s32[]{:S(2)}) async-start(), calls=%async_computation.5 | async-start | bytes 4194304 | tf_op jit(solution)/shard_map/psum | solution.py:75
  546.2 3.1 copy-start.2
  546.6 2.7 copy-start.8
  554.2 196.0 %all-reduce.18.cloned.1.call-start = ((), (), s32[]{:S(2)}) async-start(), calls=%async_computation.6 | async-start | bytes 524288 | tf_op jit(solution)/shard_map/psum | solution.py:76
  673.2 1.3 copy-start.3
  677.2 152.2 %all-reduce.20.cloned.1.call-start = ((), (), s32[]{:S(2)}) async-start(), calls=%async_computation.7 | async-start | bytes 1048576 | tf_op jit(solution)/shard_map/psum | solution.py:11
  755.3 1.3 copy-start.4
Sparse Core Ops, SparseCore 0:
  13.0 51.3 all-gather.2
  66.9 48.1 all-gather.4
  118.0 75.5 all-reduce.9
  206.9 115.3 all-reduce.11
  328.6 72.7 all-reduce.13
  468.3 73.1 all-reduce.21
  554.3 115.3 all-reduce.15
  677.3 72.7 all-reduce.17
  757.6 71.7 all-reduce.19
where the time goes:
time: 851 us; the launch traced here: 844 us
  waiting for transfers between devices  680 us (80%)
  matrix products  68.9 us (8%)
  other arithmetic  61.2 us (7%)
  local copies, waits for them, and re-layouts  15.7 us (2%)
  between operations  15.7 us (2%)
    psum x4, waiting for transfers between devices, from_root(): return lax.psum(block, axis)  327 us
    psum x1, waiting for transfers between devices, shards(): x_rows = product(lax.psum(product(updated, refl_cols), 'col'), g_inverse)  112 us
    psum x1, waiting for transfers between devices, shards(): lax.psum((product(next_panel.T, next_panel), product(picker.T, next_panel...  70.8 us
    psum x1, waiting for transfers between devices, shards(): m_core = product(g_inverse.T, lax.psum(product(refl_rows.T, x_rows), 'row'))  69.8 us
    dot_general x31, matrix products, product(): jnp.dot(left, right, precision=lax.Precision.HIGHEST, preferred_element_t...  61.7 us
    all_gather x1, waiting for transfers between devices, shards(): lax.all_gather(first_y, 'col', axis=0, tiled=True)  50.7 us
    all_gather x1, waiting for transfers between devices, shards(): lax.all_gather(l_panel, 'col', axis=0, tiled=True)  49.6 us
    another operation x6, other arithmetic, shards(): factor = jnp.linalg.cholesky(gram)  34 us
  transfers between devices with their start and end apart: 9, of which 9 were waited for; matrix products, arithmetic and copies ran while one was open for 2% of the time, Pallas kernels for 0%

commit v1 on v0

--- a/solution.py
+++ b/solution.py
@@ -42,7 +42,9 @@
     first_y = solved - half_term
     panel_out = first_y - half_term
     y_rows, l_rows = (
-        lax.all_gather(first_y, "col", axis=0, tiled=True),
+        jnp.concatenate(
+            lax.all_to_all(jnp.stack([first_y] * lax.axis_size("col")), "col", 0, 0), axis=0
+        ),
         lax.all_gather(l_panel, "col", axis=0, tiled=True),
     )
     stacked = jnp.stack(

time: 851 us -> 811 us (0.953)
  waiting for transfers between devices: 680 us -> 631 us
    all_gather x1 -> x0, waiting for transfers between devices: 50.7 us -> none  [shards(): lax.all_gather(first_y, 'col', axis=0, tiled=True)]
    all_to_all x0 -> x1, waiting for transfers between devices: none -> 26.9 us  [shards(): lax.all_to_all(jnp.stack([first_y] * lax.axis_size('col')), 'col', 0, 0)]
    all_gather x1, waiting for transfers between devices: 49.6 us -> 24.5 us  [shards(): lax.all_gather(l_panel, 'col', axis=0, tiled=True)]
  transfers between devices with their start and end apart: 9 -> 9, of which waited for: 9 -> 9; matrix products, arithmetic and copies ran while one was open for 2% -> 3% of each run, Pallas kernels for 0% -> 0%
where the time goes in v1:
time: 811 us; the launch traced here: 802 us
  waiting for transfers between devices  631 us (78%)
  matrix products  68.9 us (8%)
  other arithmetic  61.2 us (8%)
  between operations  16 us (2%)
  local copies, waits for them, and re-layouts  15.6 us (2%)
  starting transfers between devices  9.01 us (1%)
    psum x4, waiting for transfers between devices, from_root(): return lax.psum(block, axis)  327 us
    psum x1, waiting for transfers between devices, shards(): x_rows = product(lax.psum(product(updated, refl_cols), 'col'), g_inverse)  112 us
    psum x1, waiting for transfers between devices, shards(): lax.psum((product(next_panel.T, next_panel), product(picker.T, next_panel...  70.8 us
    psum x1, waiting for transfers between devices, shards(): m_core = product(g_inverse.T, lax.psum(product(refl_rows.T, x_rows), 'row'))  69.8 us
    dot_general x31, matrix products, product(): jnp.dot(left, right, precision=lax.Precision.HIGHEST, preferred_element_t...  61.7 us
    another operation x6, other arithmetic, shards(): factor = jnp.linalg.cholesky(gram)  34 us
    all_to_all x1, waiting for transfers between devices, shards(): lax.all_to_all(jnp.stack([first_y] * lax.axis_size('col')), 'col', 0, 0)  26.9 us
    all_gather x1, waiting for transfers between devices, shards(): lax.all_gather(l_panel, 'col', axis=0, tiled=True)  24.5 us
  transfers between devices with their start and end apart: 9, of which 9 were waited for; matrix products, arithmetic and copies ran while one was open for 3% of the time, Pallas kernels for 0%

profile of v1, /device:TPU:2, one launch (start us, length us, event | category | flops | bytes accessed | tf_op | source)
XLA Modules:
  0.0 802.5 jit_solution(4105660120071482601)
XLA Ops:
  7.2 0.7 all-gather.2.cloned.1.call-update
  8.1 1.3 fusion.23
  9.5 0.4 fusion.24
  9.9 1.1 fusion.3
  11.0 1.8 fusion.22
  12.8 1.6 stack.8
  14.4 7.6 all-to-all-start
  22.1 26.9 %all-to-all-done = f32[32,64,256]{2,1,0:T(8,128)S(1)} async-done(((f32[32,64,256]{2,1,0:T(8,128)}), f32[32,64,256]{2,1,0:T(8,128)S(1)}, u32[]{:S(2)}, u32[]{:S(2)}) %all-to-all-start) | async-done | bytes 2097184 | tf_op jit(solution)/shard_map/all_to_all | solution.py:46
  49.0 24.5 %all-gather.2.cloned.1.call-done = f32[2048,256]{1,0:T(8,128)} async-done(((f32[64,256]{1,0:T(8,128)}), f32[2048,256]{1,0:T(8,128)}) %all-gather.2.cloned.1.call-update) | async-done | bytes 2097168 | tf_op jit(solution)/shard_map/all_gather | solution.py:48
  73.5 1.1 dynamic-slice_bitcast_fusion
  74.6 1.0 maximum_select_fusion
  75.7 76.4 %all-reduce.10.cloned.1.call-done = f32[2,512,256]{2,1,0:T(8,128)} async-done(((f32[2,512,256]{2,1,0:T(8,128)}), f32[2,512,256]{2,1,0:T(8,128)}) %all-reduce.10.cloned.1.call-update) | async-done | bytes 1048592 | tf_op jit(solution)/shard_map/psum | solution.py:11
  152.1 4.7 fusion.7
  156.8 4.8 fusion
  161.6 2.0 copy-done.1
  163.6 1.6 slice_select_fusion
  165.5 115.1 %all-reduce.12.cloned.1.call-done = f32[2048,256]{1,0:T(8,128)} async-done(((f32[2048,256]{1,0:T(8,128)}), f32[2048,256]{1,0:T(8,128)}) %all-reduce.12.cloned.1.call-update) | async-done | bytes 2097168 | tf_op jit(solution)/shard_map/psum | solution.py:11
  280.6 1.9 broadcast_select_fusion
  282.6 4.2 fusion.25
  286.8 2.1 fusion.2
  288.9 70.8 %all-reduce.14.cloned.1.call-done = f32[256,256]{0,1:T(8,128)} async-done(((f32[256,256]{0,1:T(8,128)}), f32[256,256]{0,1:T(8,128)}) %all-reduce.14.cloned.1.call-update) | async-done | bytes 262160 | tf_op jit(solution)/shard_map/psum | solution.py:67
  359.7 1.1 copy.9
  360.8 1.0 fusion.8
  361.8 11.7 %cholesky.50 = f32[128,128]{1,0:T(8,128)S(1)} custom-call(f32[128,128]{1,0:T(8,128)S(1)} %cholesky.118), custom_call_target="Cholesky" | custom-call | tf_op jit(solution)/shard_map/jit(cholesky)/cholesky | solution.py:70
  373.6 9.8 %custom-call.16 = f32[1,128,128]{1,2,0:T(8,128)S(1)} custom-call(f32[1,128,128]{2,1,0:T(8,128)S(1)} %get-tuple-element.25), custom_call_target="InvertDiagBlocksLowerTriangular" | custom-call | tf_op jit(solution)/shard_map/jit(cholesky)/cholesky | solution.py:70
  383.9 11.7 %cholesky.105 = f32[128,128]{1,0:T(8,128)S(1)} custom-call(f32[128,128]{1,0:T(8,128)S(1)} %convolution_subtract_fusion.10), custom_call_target="Cholesky" | custom-call | tf_op jit(solution)/shard_map/jit(cholesky)/cholesky | solution.py:70
  395.6 0.7 compare_reduce_fusion
  397.7 4.2 while.1
  397.9 0.6 fusion.94
  398.5 1.3 bitcast_dynamic-update-slice_fusion.2
  399.9 0.6 fusion.94
  400.5 1.3 bitcast_dynamic-update-slice_fusion.2
  401.9 19.7 %custom-call.17 = f32[2,128,128]{1,2,0:T(8,128)S(1)} custom-call(f32[2,128,128]{2,1,0:T(8,128)S(1)} %get-tuple-element.9), custom_call_target="InvertDiagBlocksLowerTriangular" | custom-call | tf_op jit(solution)/shard_map/triangular_solve | solution.py:27
  421.5 1.1 fusion.4
  422.6 1.8 convolution_subtract_fusion
  424.5 1.1 fusion.16
  425.8 0.8 dynamic-slice_select_fusion.1
  427.0 73.0 %all-reduce.22.cloned.1.call-done = (f32[512,256]{0,1:T(8,128)}, f32[256,256]{1,0:T(8,128)}) async-done(((f32[512,256]{0,1:T(8,128)}, f32[256,256]{1,0:T(8,128)}), (f32[512,256]{0,1:T(8,128)}, f32[256,256]{1,0:T(8,128)})) %all-reduce.22.cloned.1.call-update) | async-done | bytes 786448 | tf_op jit(solution)/shard_map/psum | solution.py:11
  500.0 1.2 fusion.10
  501.2 1.3 convolution_subtract_fusion.9
  503.5 0.4 convolution_subtract_fusion.7
  504.3 0.4 convolution_subtract_fusion.6
  505.1 0.4 convolution_subtract_fusion.5
  505.9 0.4 convolution_subtract_fusion.4
  506.7 1.1 convolution_subtract_fusion.3
  507.8 4.9 fusion.26
  512.7 0.5 all-reduce.18.cloned.1.call-start
  513.2 1.3 fusion.31
  514.6 0.4 convolution_subtract_fusion.2
  515.0 0.4 fusion.32
  515.4 0.4 convolution_subtract_fusion.1
  516.1 112.1 %all-reduce.16.cloned.1.call-done = f32[2048,256]{1,0:T(8,128)} async-done(((f32[2048,256]{1,0:T(8,128)}), f32[2048,256]{1,0:T(8,128)}) %all-reduce.16.cloned.1.call-update) | async-done | bytes 2097168 | tf_op jit(solution)/shard_map/psum | solution.py:77
  628.2 3.5 fusion.34
  631.8 1.3 copy-done.3
  633.1 2.6 fusion.35
  635.9 2.9 copy.13
  638.8 69.8 %all-reduce.18.cloned.1.call-done = f32[256,256]{1,0:T(8,128)} async-done(((f32[256,256]{1,0:T(8,128)}), f32[256,256]{1,0:T(8,128)}) %all-reduce.18.cloned.1.call-update) | async-done | bytes 262160 | tf_op jit(solution)/shard_map/psum | solution.py:78
  708.7 1.3 fusion.36
  710.0 3.8 fusion.1
  713.8 1.3 copy-done.4
  715.1 0.8 dynamic-slice_select_fusion
  716.0 9.9 %fusion.37 = f32[2048,512]{1,0:T(8,128)} fusion(f32[2048,256]{0,1:T(8,128)} %copy-done.4, f32[512,256]{0,1:T(8,128)S(1)} %copy-done.7), kind=kOutput, calls=%fused_computation.84 | convolution fusion | flops 3221225472 | bytes 6815744 | tf_op jit(solution)/shard_map/dot_general | solution.py:15
  725.9 62.0 %all-reduce.20.cloned.1.call-done = f32[512,256]{0,1:T(8,128)} async-done(((f32[512,256]{0,1:T(8,128)}), f32[512,256]{0,1:T(8,128)}) %all-reduce.20.cloned.1.call-update) | async-done | bytes 524304 | tf_op jit(solution)/shard_map/psum | solution.py:11
  788.0 7.5 add_subtract_fusion
  (52 shorter events, 5.1 us)
Async XLA Ops:
  7.2 1.0 copy-start
  7.2 66.3 %all-gather.2.cloned.1.call-start = ((), (), s32[]{:S(2)}) async-start(), calls=%async_computation.1 | async-start | bytes 2162688 | tf_op jit(solution)/shard_map/all_gather | solution.py:48
  14.4 34.6 %all-to-all-start = ((f32[32,64,256]{2,1,0:T(8,128)}), f32[32,64,256]{2,1,0:T(8,128)S(1)}, u32[]{:S(2)}, u32[]{:S(2)}) async-start(f32[32,64,256]{2,1,0:T(8,128)} %stack.8), calls=%async_computation | async-start | bytes 4194304 | tf_op jit(solution)/shard_map/all_to_all | solution.py:46
  22.0 130.1 %all-reduce.10.cloned.1.call-start = ((), (), s32[]{:S(2)}) async-start(), calls=%async_computation.2 | async-start | bytes 2097152 | tf_op jit(solution)/shard_map/psum | solution.py:11
  75.7 205.0 %all-reduce.12.cloned.1.call-start = ((), (), s32[]{:S(2)}) async-start(), calls=%async_computation.3 | async-start | bytes 4194304 | tf_op jit(solution)/shard_map/psum | solution.py:11
  152.1 4.7 copy-start.5
  152.1 4.7 copy-start.6
  161.6 2.0 copy-start.1
  165.2 194.5 %all-reduce.14.cloned.1.call-start = ((), (), s32[]{:S(2)}) async-start(), calls=%async_computation.4 | async-start | bytes 524288 | tf_op jit(solution)/shard_map/psum | solution.py:67
  286.7 213.3 %all-reduce.22.cloned.1.call-start = ((), (), s32[]{:S(2)}) async-start(), calls=%async_computation.8 | async-start | bytes 1572864 | tf_op jit(solution)/shard_map/psum | solution.py:11
  426.7 201.5 %all-reduce.16.cloned.1.call-start = ((), (), s32[]{:S(2)}) async-start(), calls=%async_computation.5 | async-start | bytes 4194304 | tf_op jit(solution)/shard_map/psum | solution.py:77
  504.7 3.1 copy-start.2
  505.1 2.7 copy-start.7
  512.7 196.0 %all-reduce.18.cloned.1.call-start = ((), (), s32[]{:S(2)}) async-start(), calls=%async_computation.6 | async-start | bytes 524288 | tf_op jit(solution)/shard_map/psum | solution.py:78
  631.7 1.3 copy-start.3
  635.7 152.3 %all-reduce.20.cloned.1.call-start = ((), (), s32[]{:S(2)}) async-start(), calls=%async_computation.7 | async-start | bytes 1048576 | tf_op jit(solution)/shard_map/psum | solution.py:11
  713.8 1.3 copy-start.4
Sparse Core Ops, SparseCore 0:
  10.6 62.9 all-gather.1
  76.4 75.6 all-reduce.9
  165.4 115.2 all-reduce.11
  286.9 72.7 all-reduce.13
  426.8 73.1 all-reduce.21
  512.8 115.3 all-reduce.15
  635.8 72.8 all-reduce.17
  716.1 71.8 all-reduce.19
